TPU v7x, 512 devices: a whole 4x8x8 slice. The times are simulated.
512 devices in a mesh: wide: 64 (over z, y_lo, x), narrow: 8 (over y_hi, core).
Axes of the slice: x: 4, y: 8 (y_hi: 4, y_lo: 2; y = y_hi * 2 + y_lo), z: 8, core: 2. Of those that a mesh axis runs over, the one named last changes fastest.
Arguments:
- activation_cache: bfloat16 [64, 128, 8192], P('wide', None, 'narrow'), may hold values from -6 to 6
- token_ids: int32 [64, 128], P('wide'), may hold values from 0 to 127
- cotangent: bfloat16 [64, 128, 37120], P('wide', None, 'narrow'), may hold values from -6 to 6
- adapter_b: float32 [64, 16, 8192], P('wide', None, 'narrow'), may hold values from -4 to 4
- first_b: float32 [64, 16, 8192], P('wide', None, 'narrow'), may hold values from -0.3 to 0.3
- second_b: float32 [64, 16, 8192], P('wide', None, 'narrow'), may hold values from 0.0001 to 0.002
- adapter_a: float32 [64, 16, 37120], P('wide', None, 'narrow'), may hold values from -4 to 4
- first_a: float32 [64, 16, 37120], P('wide', None, 'narrow'), may hold values from -0.3 to 0.3
- second_a: float32 [64, 16, 37120], P('wide', None, 'narrow'), may hold values from 0.0001 to 0.002
- resident: bfloat16 [8192, 37120], P('narrow', 'wide'), may hold values from -6 to 6
- block_owner: int32 [64], replicated, may hold values from 0 to 63, each once
- next_rows: bfloat16 [512, 8192], P('wide', 'narrow'), may hold values from -6 to 6
Outputs:
- merged: bfloat16 [8192, 37120], P('narrow', 'wide')
- projected: bfloat16 [512, 37120], P('narrow', 'wide')
Inputs may be any that keep to these rules, and one draw needn't show every extreme that they name: `block_owner`: each column block is stored at exactly one position.
All inputs are finite; a program needn't handle non-finite values.
Results may differ from a plain program's by a relative error of at most 0.0058.
Values may be sent and summed in bfloat16 or wider, within the bound.
A program may use at most 64 MiB of HBM per device.

v0:
```python
import math

import jax
import jax.numpy as jnp
from jax import lax
from jax.sharding import PartitionSpec as P

D = 8192
WORKER_TOKENS = 128


adapter_scale = 4.0
rate = 0.2
beta_one = 0.9
beta_two = 0.999
bias_one = 1.0 - 0.9**20
bias_two = 1.0 - 0.999**20
eps_adam = 1e-08


def adam_step(param, first, second, grad):
    first_new = beta_one * first + (1.0 - beta_one) * grad
    second_new = beta_two * second + (1.0 - beta_two) * grad * grad
    update = first_new / bias_one / (jnp.sqrt(second_new / bias_two) + eps_adam)
    return (param - rate * update).astype(jnp.bfloat16)


def per_device(
    activation_cache,
    token_ids,
    cotangent,
    adapter_b,
    first_b,
    second_b,
    adapter_a,
    first_a,
    second_a,
    resident,
    block_owner,
    next_rows,
):
    inverse_root = 1.0 / math.sqrt(D)
    highest_precision = lax.Precision.HIGHEST
    worker_group = lax.axis_size("wide")
    block_cols = resident.shape[1]
    selected_rows = jnp.take(activation_cache[0], token_ids[0], axis=0).astype(jnp.float32)
    incoming_gradient = cotangent[0].astype(jnp.float32)
    factor_b = adapter_b[0]
    factor_a = adapter_a[0]
    part_hidden = jnp.dot(selected_rows, factor_b.T, precision=highest_precision)
    part_upstream = jnp.dot(incoming_gradient, factor_a.T, precision=highest_precision)
    hidden_state, upstream_gradient = lax.psum((part_hidden, part_upstream), "narrow")
    hidden_state = hidden_state * inverse_root
    gradient_left = (
        adapter_scale
        / WORKER_TOKENS
        * jnp.dot(hidden_state.T, incoming_gradient, precision=highest_precision)
    )
    gradient_right = (
        adapter_scale
        * inverse_root
        / WORKER_TOKENS
        * jnp.dot(upstream_gradient.T, selected_rows, precision=highest_precision)
    )
    new_b = adam_step(factor_b, first_b[0], second_b[0], gradient_right)
    new_a = adam_step(factor_a, first_a[0], second_a[0], gradient_left)
    full_a = lax.all_gather(new_a, "narrow", axis=1, tiled=True)
    blocks = full_a.reshape(full_a.shape[0], worker_group, block_cols)
    ordered = jnp.take(blocks, block_owner, axis=1)
    arrived = lax.all_to_all(ordered, "wide", split_axis=1, concat_axis=0, tiled=True)
    right_rows = arrived.reshape(worker_group * full_a.shape[0], block_cols)
    weight_change = lax.dot_general(
        lax.all_gather(new_b, "wide", axis=0, tiled=True),
        right_rows,
        (((0,), (0,)), ((), ())),
        preferred_element_type=jnp.float32,
    )
    merged = (resident.astype(jnp.float32) + adapter_scale / worker_group * weight_change).astype(
        jnp.bfloat16
    )
    all_next = lax.all_gather(next_rows, "wide", axis=0, tiled=True)
    summed = lax.psum_scatter(
        jnp.dot(all_next, merged, preferred_element_type=jnp.float32),
        "narrow",
        scatter_dimension=0,
        tiled=True,
    )
    projected = (summed * inverse_root).astype(jnp.bfloat16)
    return (merged, projected)


def solution(mesh):
    return jax.shard_map(
        per_device,
        mesh=mesh,
        in_specs=(
            P("wide", None, "narrow"),
            P("wide", None),
            P("wide", None, "narrow"),
            P("wide", None, "narrow"),
            P("wide", None, "narrow"),
            P("wide", None, "narrow"),
            P("wide", None, "narrow"),
            P("wide", None, "narrow"),
            P("wide", None, "narrow"),
            P("narrow", "wide"),
            P(),
            P("wide", "narrow"),
        ),
        out_specs=(P("narrow", "wide"), P("narrow", "wide")),
        check_vma=False,
    )
```

profile of v0, /device:TPU:1, one launch (start us, length us, event | category | flops | bytes accessed | tf_op | source)
XLA Modules:
  0.0 737.8 jit_solution(15029507416421847108)
XLA Ops:
  7.2 0.0 copy-start
  7.2 0.0 copy-start.1
  7.2 0.0 all-gather.9.cloned.1.call-start
  7.2 0.8 fusion.33
  8.0 0.7 compare_and_fusion.1
  8.7 2.0 gather_fusion
  10.7 0.0 copy-done
  10.7 0.0 copy-done.1
  10.7 0.0 copy-start.4
  10.7 0.0 copy-start.2
  10.7 0.0 copy-start.3
  10.8 0.6 fusion.2
  11.4 0.2 copy-done.4
  11.6 0.4 fusion.20
  11.9 29.6 %all-reduce = (f32[128,16]{0,1:T(8,128)S(1)}, f32[128,16]{0,1:T(8,128)S(1)}) all-reduce(f32[128,16]{0,1:T(8,128)S(1)} %fusion.2, f32[128,16]{0,1:T(8,128)S(1)} %fusion.20), channel_id=1, replica_groups=mesh['wide'=64,'narrow'=8] {'narrow'}, use_global_device_ids=true, to_apply=%region_0.1 | all-reduce | flops 4096 | bytes 32768 | tf_op jit(solution)/shard_map/psum | solution.py:52
  41.5 0.0 copy-done.2
  41.5 0.0 copy-done.3
  41.5 0.0 copy-start.5
  41.5 0.0 copy-start.7
  41.5 1.7 fusion.17
  43.3 0.0 all-gather.9.cloned.1.call-update
  43.3 0.0 all-gather.5.cloned.1.call-start
  43.4 0.0 copy-done.5
  43.4 0.0 copy-done.6
  43.4 1.0 fusion.30
  44.3 0.0 all-gather.5.cloned.1.call-update
  44.4 0.0 copy-done.7
  44.4 35.4 %all-gather.9.cloned.1.call-done = bf16[8,4640,16]{1,2,0:T(8,128)(2,1)} async-done(((bf16[1,4640,16]{1,2,0:T(8,128)(2,1)}), bf16[8,4640,16]{1,2,0:T(8,128)(2,1)}) %all-gather.9.cloned.1.call-update) | async-done | bytes 1187856 | tf_op jit(solution)/shard_map/all_gather | solution.py:67
  79.8 1.5 copy.18
  81.3 1.9 reshape.78
  83.2 4.8 reshape.58
  88.0 2.1 copy.19
  90.0 1.8 gather_fusion.1
  91.8 2.6 select_bitcast_fusion
  94.4 11.5 %all-to-all-start = ((bf16[16,64,580]{2,0,1:T(8,128)(2,1)}), bf16[16,64,580]{2,0,1:T(8,128)(2,1)S(1)}, u32[]{:S(2)}, u32[]{:S(2)}) async-start(bf16[16,64,580]{2,0,1:T(8,128)(2,1)} %select_bitcast_fusion), calls=%async_computation | async-start | bytes 2621440 | tf_op jit(solution)/shard_map/all_to_all | solution.py:70
  105.9 0.0 all-gather.7.cloned.1.call-start
  106.0 0.7 all-gather.7.cloned.1.call-update
  106.6 0.0 reduce-scatter.4.cloned.1.call-start
  106.7 234.2 %all-gather.5.cloned.1.call-done = bf16[1024,1024]{1,0:T(8,128)(2,1)} async-done(((bf16[16,1024]{1,0:T(8,128)(2,1)}), bf16[1024,1024]{1,0:T(8,128)(2,1)}) %all-gather.5.cloned.1.call-update) | async-done | bytes 2097168 | tf_op jit(solution)/shard_map/all_gather | solution.py:73
  340.9 0.0 all-to-all-done
  340.9 4.4 add_convert_fusion
  345.3 294.0 %all-gather.7.cloned.1.call-done = bf16[512,1024]{1,0:T(8,128)(2,1)} async-done(((bf16[8,1024]{1,0:T(8,128)(2,1)}), bf16[512,1024]{1,0:T(8,128)(2,1)}) %all-gather.7.cloned.1.call-update) | async-done | bytes 1048592 | tf_op jit(solution)/shard_map/all_gather | solution.py:81
  639.3 2.4 convolution_bitcast_fusion
  641.7 1.5 copy.21
  643.2 0.0 reduce-scatter.4.cloned.1.call-update
  643.2 86.2 %reduce-scatter.4.cloned.1.call-done = f32[64,580]{1,0:T(8,128)} async-done(((f32[512,580]{1,0:T(8,128)}), f32[64,580]{1,0:T(8,128)}) %reduce-scatter.4.cloned.1.call-update) | async-done | bytes 148496
  729.4 1.1 copy.22
  730.5 0.8 copy.20
  (6 shorter events, 0.1 us)
Async XLA Ops:
  7.2 3.5 copy-start
  7.2 3.5 copy-start.1
  7.2 72.6 %all-gather.9.cloned.1.call-start = ((), (), s32[]{:S(2)}) async-start(), calls=%async_computation.4 | async-start | bytes 1363968 | tf_op jit(solution)/shard_map/all_gather | solution.py:67
  10.7 0.8 copy-start.4
  10.7 30.8 %copy-start.2 = (f32[1,16,4640]{2,1,0:T(8,128)S(1)}, f32[1,16,4640]{2,1,0:T(8,128)}, u32[]{:S(2)}) copy-start(f32[1,16,4640]{2,1,0:T(8,128)} %param.20) | copy-start | bytes 890884
  10.7 30.8 %copy-start.3 = (f32[1,16,4640]{2,1,0:T(8,128)S(1)}, f32[1,16,4640]{2,1,0:T(8,128)}, u32[]{:S(2)}) copy-start(f32[1,16,4640]{2,1,0:T(8,128)} %param.19) | copy-start | bytes 890884
  41.5 1.8 copy-start.5
  41.5 1.9 copy-start.6
  41.5 2.8 copy-start.7
  43.3 297.6 %all-gather.5.cloned.1.call-start = ((), (), s32[]{:S(2)}) async-start(), calls=%async_computation.2 | async-start | bytes 2129920 | tf_op jit(solution)/shard_map/all_gather | solution.py:73
  94.4 246.5 %all-to-all-start = ((bf16[16,64,580]{2,0,1:T(8,128)(2,1)}), bf16[16,64,580]{2,0,1:T(8,128)(2,1)S(1)}, u32[]{:S(2)}, u32[]{:S(2)}) async-start(bf16[16,64,580]{2,0,1:T(8,128)(2,1)} %select_bitcast_fusion), calls=%async_computation | async-start | bytes 2621440 | tf_op jit(solution)/shard_map/all_to_all | solution.py:70
  105.9 533.4 %all-gather.7.cloned.1.call-start = ((), (), s32[]{:S(2)}) async-start(), calls=%async_computation.3 | async-start | bytes 1064960 | tf_op jit(solution)/shard_map/all_gather | solution.py:81
  106.6 622.7 %reduce-scatter.4.cloned.1.call-start = ((), (), s32[]{:S(2)}) async-start(), calls=%async_computation.5 | async-start | bytes 1474560
Sparse Core Ops, SparseCore 0:
  43.4 36.3 all-gather.8
  82.4 258.4 all-gather.4
  343.0 296.2 all-gather.6
  643.3 86.0 reduce-scatter.3
where the time goes:
time: 739 us; the launch traced here: 738 us
  waiting for transfers between devices  650 us (88%)
  blocking collectives  29.6 us (4%)
  local copies, waits for them, and re-layouts  17.6 us (2%)
  between operations  13.9 us (2%)
  starting transfers between devices  11.6 us (2%)
  matrix products  10.5 us (1%)
    all_gather x1, waiting for transfers between devices, per_device(): all_next = lax.all_gather(next_rows, 'wide', axis=0, tiled=True)  294 us
    all_gather x1, waiting for transfers between devices, per_device(): lax.all_gather(new_b, 'wide', axis=0, tiled=True)  234 us
    unnamed x5, waiting for transfers between devices  86.9 us
    all_gather x1, waiting for transfers between devices, per_device(): full_a = lax.all_gather(new_a, 'narrow', axis=1, tiled=True)  35.4 us
    psum x1, blocking collectives, per_device(): lax.psum((part_hidden, part_upstream), 'narrow')  29.6 us
  transfers between devices with their start and end apart: 5, of which 4 were waited for; matrix products, arithmetic and copies ran while one was open for 3% of the time, Pallas kernels for 0%

commit v1 on v0

v1 whole, which is shorter than its diff:
```python
import math

import jax
import jax.numpy as jnp
from jax import lax
from jax.experimental import pallas as pl
from jax.experimental.pallas import tpu as pltpu
from jax.sharding import PartitionSpec as P

D = 8192
WORKER_TOKENS = 128
F32 = jnp.float32
BF16 = jnp.bfloat16
MESH = pl.DeviceIdType.MESH

adapter_scale = 4.0
rate = 0.2
beta_one = 0.9
beta_two = 0.999
bias_one = 1.0 - 0.9**20
bias_two = 1.0 - 0.999**20
eps_adam = 1e-08

NZ, NY, NX = 8, 2, 4
LANE = 128


def adam_step(param, first, second, grad):
    first_new = beta_one * first + (1.0 - beta_one) * grad
    second_new = beta_two * second + (1.0 - beta_two) * grad * grad
    update = first_new / bias_one / (jnp.sqrt(second_new / bias_two) + eps_adam)
    return param - rate * update


def split3(v):
    hi = v.astype(BF16)
    rest = v - hi.astype(F32)
    mid = rest.astype(BF16)
    low = (rest - mid.astype(F32)).astype(BF16)
    return jnp.concatenate([hi, mid, low], axis=0)


def sum3(v):
    n = v.shape[0] // 3
    return v[:n] + v[n : 2 * n] + v[2 * n :]


def dot(a, b):
    return lax.dot_general(a, b, (((1,), (0,)), ((), ())), preferred_element_type=F32)


def dot_nt(a, b):
    return lax.dot_general(a, b, (((1,), (1,)), ((), ())), preferred_element_type=F32)


class Gather:
    def __init__(self, ref, lanes, rs, ss, first, pos, n):
        self.ref, self.lanes, self.rs, self.ss, self.n = ref, lanes, rs, ss, n
        self.z, self.y, self.x = pos
        self.first = first
        self.na, self.nb = (NX, NZ) if first == "x" else (NZ, NX)
        self.a, self.b = (self.x, self.z) if first == "x" else (self.z, self.x)

    def index(self, y, a, b):
        z, x = (b, a) if self.first == "x" else (a, b)
        return (z * NY + y) * NX + x

    def view(self, v):
        if self.lanes is None:
            return self.ref.at[v]
        return self.ref.at[v, :, self.lanes]

    def copy(self, v, dest):
        return pltpu.make_async_remote_copy(
            self.view(v), self.view(v), self.ss, self.rs.at[v], device_id=(dest, self.n), device_id_type=MESH
        )

    def to_a(self, v, d):
        self.copy(v, self.index(self.y, (self.a + d + self.na) % self.na, self.b)).start()

    def to_b(self, v, d):
        self.copy(v, self.index(self.y, self.a, (self.b + d + self.nb) % self.nb)).start()

    def arrived(self, v):
        self.copy(v, self.index(1 - self.y, self.a, self.b)).wait_recv()

    def begin(self):
        me = self.index(self.y, self.a, self.b)
        self.copy(me, self.index(1 - self.y, self.a, self.b)).start()
        self.spread(me)

    def spread(self, v):
        self.to_a(v, 1)
        self.to_a(v, -1)
        self.to_b(v, 1)
        self.to_b(v, -1)

    def pair(self):
        v = self.index(1 - self.y, self.a, self.b)
        self.arrived(v)
        self.spread(v)

    def ring_a(self, s):
        for y in range(NY):
            for way in (1, -1):
                lim = self.na // 2 - (y == (1 if way == 1 else 0))
                if s <= lim:
                    v = self.index(y, (self.a - way * s + self.na) % self.na, self.b)
                    self.arrived(v)
                    if s < lim:
                        self.to_a(v, way)
                    self.to_b(v, 1)
                    self.to_b(v, -1)

    def ring_b(self, s):
        def step(q, _):
            for y in range(NY):
                for way in (1, -1):
                    lim = self.nb // 2 - (y == (1 if way == 1 else 0))
                    if s <= lim:
                        v = self.index(y, q, (self.b - way * s + self.nb) % self.nb)
                        self.arrived(v)
                        if s < lim:
                            self.to_b(v, way)
            return 0

        lax.fori_loop(0, self.na, step, 0)

    def sent(self):
        count = self.ref.shape[0] - 1
        if self.lanes is None:
            r = self.ref.at[pl.ds(0, count)]
        else:
            r = self.ref.at[pl.ds(0, count), :, self.lanes]
        pltpu.make_async_copy(r, r, self.ss).wait()


def kernel(
    tok_ref, owner_ref, cache_h, cot_h, ab_h, fb_h, sb_h, aa_h, fa_h, sa_h, res_h, nxt_h,
    merged_h, proj_h,
    cache, cot, ab, fb, sb, aa, fa, sa, res,
    pb, gb, gn, na, s1, bl, st, af, nbt, nrc, mg, px, pxr, po, rsrc, rrcv, pj,
    in_sem, pb_s, pb_r, gb0_r, gb1_r, gn_r, g_s, s1_s, s1_r, s2_s, s2_r, s3_s, s3_r, px_s, px_r, rr_s, rr_r, loc_s,
):
    w = lax.axis_index("wide")
    n = lax.axis_index("narrow")
    x = w % NX
    y = (w // NX) % NY
    z = w // (NX * NY)
    yh = n // 2
    c = n % 2
    nw = NZ * NY * NX
    inverse_root = 1.0 / math.sqrt(D)

    bar = pltpu.get_barrier_semaphore()

    def sig_w(d, _):
        pl.semaphore_signal(bar, inc=1, device_id=((w + d) % nw, n), device_id_type=MESH)
        return 0

    def sig_n(d, _):
        pl.semaphore_signal(bar, inc=1, device_id=(w, (n + d) % 8), device_id_type=MESH)
        return 0

    lax.fori_loop(1, nw, sig_w, 0)
    lax.fori_loop(1, 8, sig_n, 0)

    loads = {}
    pairs = (
        ("ab", ab_h.at[0], ab), ("cache", cache_h.at[0], cache), ("aa", aa_h.at[0], aa), ("cot", cot_h.at[0], cot),
        ("nxt", nxt_h, gn.at[w]), ("fb", fb_h.at[0], fb), ("sb", sb_h.at[0], sb), ("fa", fa_h.at[0], fa),
        ("sa", sa_h.at[0], sa), ("res", res_h, res),
    )
    for i, (name, src, dst) in enumerate(pairs):
        loads[name] = pltpu.make_async_copy(src, dst, in_sem.at[i])
        loads[name].start()

    oht = (lax.broadcasted_iota(jnp.int32, (128, 128), 0) == tok_ref[...]).astype(F32).astype(BF16)
    loads["ab"].wait()
    loads["cache"].wait()
    hp = sum3(dot_nt(split3(ab[...]), cache[...]))
    ht = sum3(dot(split3(hp), oht))
    loads["aa"].wait()
    loads["cot"].wait()
    ut = sum3(dot_nt(split3(aa[...]), cot[...]))
    qp = sum3(dot_nt(split3(ut), oht))
    pb[n] = jnp.concatenate([ht, qp], axis=0)

    pl.semaphore_wait(bar, nw - 1 + 7)

    def pb_copy(d):
        return pltpu.make_async_remote_copy(
            pb.at[n], pb.at[n], pb_s, pb_r, device_id=(w, (n + d) % 8), device_id_type=MESH
        )

    def pb_send(d, _):
        pb_copy(d).start()
        return 0

    lax.fori_loop(1, 8, pb_send, 0)

    pos = (z, y, x)
    gath_n = Gather(gn, None, gn_r, g_s.at[0], "z", pos, n)
    gath_0 = Gather(gb, pl.ds(0, 512), gb0_r, g_s.at[1], "z", pos, n)
    gath_1 = Gather(gb, pl.ds(512, 512), gb1_r, g_s.at[2], "x", pos, n)

    loads["nxt"].wait()
    gath_n.begin()
    gath_n.pair()

    r7 = pb.at[pl.ds(0, 7)]
    pltpu.make_async_copy(r7, r7, pb_r).wait()
    total = pb[0]
    for i in range(1, 8):
        total = total + pb[i]
    hid = total[:16] * inverse_root
    qsum = total[16:]

    grad_b = adapter_scale * inverse_root / WORKER_TOKENS * sum3(dot(split3(qsum), cache[...]))
    loads["fb"].wait()
    loads["sb"].wait()
    gb[w] = adam_step(ab[...], fb[...], sb[...], grad_b).astype(BF16)
    gath_0.begin()
    gath_1.begin()

    hs = split3(hid)
    loads["fa"].wait()
    loads["sa"].wait()
    cols = cot.shape[1]
    na[:, 4608:] = jnp.zeros((16, 128), F32)
    edges = (0, 1152, 2304, 3456, cols)
    for lo, hi in zip(edges[:-1], edges[1:]):
        grad_a = adapter_scale / WORKER_TOKENS * sum3(dot(hs, cot[:, lo:hi]))
        na[:, lo:hi] = adam_step(aa[:, lo:hi], fa[:, lo:hi], sa[:, lo:hi], grad_a)
    fbk = cols // 8
    for k in range(8):
        base = fbk * k // LANE * LANE
        shift = fbk * k - base
        win = na[:, base : base + 768]
        if shift:
            win = pltpu.roll(win, 768 - shift, 1)
        blk = win[:, :640].astype(BF16)
        for t in range(5):
            s1[t, k] = blk[:, t * LANE : (t + 1) * LANE]

    own8 = pl.ds(n * 8, 8)
    holders = ((0, 0), (1, 2), (2, 4), (3, 6), (4, 1), (4, 5))

    def s1_copy(i):
        t, dest = holders[i]
        return pltpu.make_async_remote_copy(
            s1.at[t], bl.at[own8], s1_s.at[i], s1_r, device_id=(w, dest), device_id_type=MESH
        )

    for i, (t, dest) in enumerate(holders):

        @pl.when(n != dest)
        def _():
            s1_copy(i).start()

        @pl.when(n == dest)
        def _():
            bl[own8] = s1[t]

    gath_0.pair()
    gath_1.pair()
    gath_n.ring_a(1)
    gath_0.ring_a(1)
    gath_1.ring_a(1)
    gath_n.ring_a(2)
    gath_0.ring_a(2)
    gath_1.ring_a(2)

    even = c == 0
    holds = jnp.logical_or(even, jnp.logical_or(n == 1, n == 5))
    y4 = n // 4
    gets = jnp.logical_or(even, jnp.logical_or(jnp.logical_and(n == 1, y == 0), jnp.logical_and(n == 5, y == 1)))
    tile = jnp.where(even, yh, 4)

    @pl.when(holds)
    def _():
        r = bl.at[pl.ds(0, 56)]
        pltpu.make_async_copy(r, r, s1_r).wait()

        def pick(j, _):
            st[j] = bl[owner_ref[j]]
            return 0

        lax.fori_loop(0, nw, pick, 0)

    lane = pl.ds(pl.multiple_of(tile * LANE, LANE), LANE)

    def s2_copy(j):
        return pltpu.make_async_remote_copy(
            st.at[j], af.at[w, :, lane], s2_s, s2_r, device_id=(j, n), device_id_type=MESH
        )

    @pl.when(even)
    def _():
        def send(d, _):
            s2_copy((w + d) % nw).start()
            return 0

        lax.fori_loop(1, nw, send, 0)

    @pl.when(jnp.logical_and(holds, jnp.logical_not(even)))
    def _():
        def send(d, _):
            j = (w + d) % nw

            @pl.when((j // NX) % NY == y4)
            def _():
                s2_copy(j).start()

            return 0

        lax.fori_loop(1, nw, send, 0)

    @pl.when(gets)
    def _():
        own = pltpu.make_async_copy(st.at[w], af.at[w, :, lane], loc_s)
        own.start()
        own.wait()

    gath_n.ring_a(3)
    gath_0.ring_a(3)
    gath_n.ring_a(4)
    gath_0.ring_a(4)
    gath_1.ring_b(1)
    gath_n.ring_b(1)
    gath_0.ring_b(1)
    gath_1.ring_b(2)

    @pl.when(gets)
    def _():
        r = af.at[pl.ds(0, nw - 1), :, lane]
        pltpu.make_async_copy(r, r, s2_r).wait()

    def piece(t, half):
        return af.at[pl.ds(half * (nw // 2), nw // 2), :, pl.ds(pl.multiple_of(t * LANE, LANE), LANE)]

    up, down, far = (yh + 1) % 4, (yh + 3) % 4, (yh + 2) % 4

    def s3(t, half, slot, sem, dest):
        return pltpu.make_async_remote_copy(
            piece(t, half), piece(t, half), s3_s.at[sem], s3_r.at[slot], device_id=(w, dest), device_id_type=MESH
        )

    partner = yh * 2 + 1 - c
    d4 = (yh - 2 * y + 4) % 4
    even_sends = (
        (yh, 0, 2, 0, up * 2), (yh, 1, 5, 1, down * 2), (yh, 1, 3, 2, up * 2), (yh, 0, 4, 3, down * 2),
        (yh, 0, 0, 4, partner), (yh, 1, 1, 5, partner),
    )
    src_sends = (
        (4, 0, 8, 0, up * 2 + 1), (4, 1, 9, 1, down * 2 + 1), (4, 1, 9, 2, up * 2 + 1), (4, 0, 8, 3, down * 2 + 1),
        (4, 0, 8, 4, partner), (4, 1, 9, 5, partner),
    )

    @pl.when(even)
    def _():
        for args in even_sends:
            s3(*args).start()

    @pl.when(jnp.logical_and(c == 1, d4 == 0))
    def _():
        for args in src_sends:
            s3(*args).start()

    gath_n.ring_b(2)
    gath_0.ring_b(2)

    @pl.when(even)
    def _():
        s3(down, 0, 2, 0, partner).wait_recv()
        s3(down, 0, 6, 6, up * 2).start()
        s3(down, 0, 2, 7, partner).start()
        s3(up, 1, 5, 0, partner).wait_recv()
        s3(up, 1, 7, 8, down * 2).start()
        s3(up, 1, 5, 9, partner).start()

    @pl.when(jnp.logical_and(c == 1, d4 == 1))
    def _():
        s3(4, 0, 8, 0, partner).wait_recv()
        s3(4, 0, 8, 0, up * 2 + 1).start()
        s3(4, 0, 8, 1, partner).start()
        s3(4, 1, 9, 0, partner).wait_recv()
        s3(4, 1, 9, 2, partner).start()

    @pl.when(jnp.logical_and(c == 1, d4 == 3))
    def _():
        s3(4, 1, 9, 0, partner).wait_recv()
        s3(4, 1, 9, 0, down * 2 + 1).start()
        s3(4, 1, 9, 1, partner).start()
        s3(4, 0, 8, 0, partner).wait_recv()
        s3(4, 0, 8, 2, partner).start()

    @pl.when(even)
    def _():
        s3(down, 1, 3, 0, partner).wait_recv()
        s3(down, 1, 3, 10, partner).start()
        s3(up, 0, 4, 0, partner).wait_recv()
        s3(up, 0, 4, 11, partner).start()

    gath_1.ring_b(3)
    gath_1.ring_b(4)

    for h in range(4):
        for k in range(2):
            i = 2 * h + k
            rows = gn[pl.ds(i * 8, 8)].astype(F32).reshape(64, gn.shape[2]).astype(BF16)
            nrc[k, h * 64 : (h + 1) * 64] = rows

    for t in range(8):
        part = gb[:, :, t * LANE : (t + 1) * LANE].reshape(nw * 16, LANE)
        nbt[t * LANE : (t + 1) * LANE, :] = part.T

    @pl.when(even)
    def _():
        s3(far, 0, 6, 0, partner).wait_recv()
        s3(far, 0, 6, 12, partner).start()
        s3(far, 1, 7, 0, partner).wait_recv()
        s3(far, 1, 7, 13, partner).start()
        s3(4, 0, 8, 0, partner).wait_recv()
        s3(4, 1, 9, 0, partner).wait_recv()

    @pl.when(jnp.logical_and(c == 1, d4 == 2))
    def _():
        s3(4, 0, 8, 0, partner).wait_recv()
        s3(4, 0, 8, 0, partner).start()
        s3(4, 1, 9, 0, partner).wait_recv()
        s3(4, 1, 9, 1, partner).start()

    @pl.when(c == 1)
    def _():
        for t, half, slot in (
            (yh, 0, 0), (yh, 1, 1), (down, 0, 2), (down, 1, 3), (up, 0, 4), (up, 1, 5), (far, 0, 6), (far, 1, 7),
        ):
            s3(t, half, slot, 0, partner).wait_recv()

    fbw = res.shape[1]
    loads["res"].wait()

    def merge(t, _):
        rows = pl.ds(pl.multiple_of(t * 128, 128), 128)
        delta = dot(nbt[rows, :], af[...].reshape(nw * 16, 640))
        mg[rows, :] = (res[rows, :].astype(F32) + adapter_scale / nw * delta[:, :fbw]).astype(BF16)
        return 0

    lax.fori_loop(0, res.shape[0] // 128, merge, 0)
    out_m = pltpu.make_async_copy(mg, merged_h, in_sem.at[0])
    out_m.start()

    px[...] = dot(nrc[1 - c], mg[...]).astype(BF16)
    xcopy = pltpu.make_async_remote_copy(px, pxr, px_s, px_r, device_id=(w, partner), device_id_type=MESH)
    xcopy.start()
    po[...] = dot(nrc[c], mg[...]).reshape(po.shape)
    xcopy.wait_recv()
    for h in range(4):
        both = po[h] + pxr[h * 64 : (h + 1) * 64].astype(F32)
        po[h] = both
        rsrc[h] = both.astype(BF16)

    def rr_copy(d):
        h = (yh + d) % 4
        return pltpu.make_async_remote_copy(
            rsrc.at[h], rrcv.at[yh], rr_s.at[d], rr_r, device_id=(w, h * 2 + c), device_id_type=MESH
        )

    for d in (2, 1, 3):
        rr_copy(d).start()
    r3 = rrcv.at[pl.ds(0, 3)]
    pltpu.make_async_copy(r3, r3, rr_r).wait()
    acc = po[yh]
    for d in (1, 2, 3):
        acc = acc + rrcv[(yh + d) % 4].astype(F32)
    pj[...] = (acc * inverse_root).astype(BF16)
    out_p = pltpu.make_async_copy(pj, proj_h, in_sem.at[1])
    out_p.start()

    pltpu.make_async_copy(r7, r7, pb_s).wait()
    gath_n.sent()
    gath_0.sent()
    gath_1.sent()
    for i, (t, dest) in enumerate(holders):

        @pl.when(n != dest)
        def _():
            s1_copy(i).wait_send()

    @pl.when(even)
    def _():
        r = st.at[pl.ds(0, nw - 1)]
        pltpu.make_async_copy(r, r, s2_s).wait()
        for i in range(14):
            s3(0, 0, 0, i, partner).wait_send()

    @pl.when(jnp.logical_and(holds, jnp.logical_not(even)))
    def _():
        @pl.when(gets)
        def _():
            r = st.at[pl.ds(0, nw // 2 - 1)]
            pltpu.make_async_copy(r, r, s2_s).wait()

        @pl.when(jnp.logical_not(gets))
        def _():
            r = st.at[pl.ds(0, nw // 2)]
            pltpu.make_async_copy(r, r, s2_s).wait()

    @pl.when(c == 1)
    def _():
        for i in range(2):
            s3(0, 0, 0, i, partner).wait_send()

        @pl.when(d4 != 2)
        def _():
            s3(0, 0, 0, 2, partner).wait_send()

        @pl.when(d4 == 0)
        def _():
            for i in range(3, 6):
                s3(0, 0, 0, i, partner).wait_send()

    xcopy.wait_send()
    for d in (2, 1, 3):
        rr_copy(d).wait_send()
    out_m.wait()
    out_p.wait()


def per_device(
    activation_cache, token_ids, cotangent, adapter_b, first_b, second_b, adapter_a, first_a, second_a, resident,
    block_owner, next_rows,
):
    dl = activation_cache.shape[2]
    cl = cotangent.shape[2]
    rl, fb = resident.shape
    nw = NZ * NY * NX
    anyspec = pl.BlockSpec(memory_space=pl.ANY)
    dma = pltpu.SemaphoreType.DMA
    vm = pltpu.VMEM
    scratch = [
        vm((128, dl), BF16), vm((128, cl), BF16), vm((16, dl), F32), vm((16, dl), F32), vm((16, dl), F32),
        vm((16, cl), F32), vm((16, cl), F32), vm((16, cl), F32), vm((rl, fb), BF16),
        vm((8, 32, 128), F32),
        vm((nw, 16, dl), BF16),
        vm((nw, 8, dl), BF16),
        vm((16, 4736), F32),
        vm((5, 8, 16, LANE), BF16),
        vm((nw, 16, LANE), BF16),
        vm((nw, 16, LANE), BF16),
        vm((nw, 16, 640), BF16),
        vm((dl, nw * 16), BF16),
        vm((2, 256, dl), BF16),
        vm((rl, fb), BF16),
        vm((256, fb), BF16), vm((256, fb), BF16),
        vm((4, 64, fb), F32),
        vm((4, 64, fb), BF16), vm((4, 64, fb), BF16),
        vm((64, fb), BF16),
        dma((10,)), dma(()), dma(()),
        dma((nw,)), dma((nw,)), dma((nw,)), dma((3,)),
        dma((6,)), dma(()), dma(()), dma(()),
        dma((14,)), dma((10,)),
        dma(()), dma(()), dma((4,)), dma(()), dma(()),
    ]
    return pl.pallas_call(
        kernel,
        out_shape=(jax.ShapeDtypeStruct((rl, fb), BF16), jax.ShapeDtypeStruct((64, fb), BF16)),
        in_specs=[pl.BlockSpec(memory_space=pltpu.VMEM), pl.BlockSpec(memory_space=pltpu.SMEM)] + [anyspec] * 10,
        out_specs=(anyspec, anyspec),
        scratch_shapes=scratch,
        compiler_params=pltpu.CompilerParams(collective_id=0, has_side_effects=True, vmem_limit_bytes=60 * 1024 * 1024),
        name="merge_step",
    )(
        token_ids, block_owner, activation_cache, cotangent, adapter_b, first_b, second_b, adapter_a, first_a, second_a,
        resident, next_rows,
    )


def solution(mesh):
    return jax.shard_map(
        per_device,
        mesh=mesh,
        in_specs=(
            P("wide", None, "narrow"),
            P("wide", None),
            P("wide", None, "narrow"),
            P("wide", None, "narrow"),
            P("wide", None, "narrow"),
            P("wide", None, "narrow"),
            P("wide", None, "narrow"),
            P("wide", None, "narrow"),
            P("wide", None, "narrow"),
            P("narrow", "wide"),
            P(),
            P("wide", "narrow"),
        ),
        out_specs=(P("narrow", "wide"), P("narrow", "wide")),
        check_vma=False,
    )
```

time: 739 us -> 88.7 us (0.12)
  waiting for transfers between devices: 650 us -> 0 us
  Pallas kernels: 0 us -> 80.9 us
  blocking collectives: 29.6 us -> 0 us
  between operations: 13.9 us -> 0.66 us
  starting transfers between devices: 11.6 us -> 0 us
  local copies, waits for them, and re-layouts: 17.6 us -> 7.02 us
  matrix products: 10.5 us -> 0 us
    all_gather x3 -> x0, waiting for transfers between devices: 564 us -> none  [the longest x1 294 us: per_device(): all_next = lax.all_gather(next_rows, 'wide', axis=0, tiled=True)]
    unnamed x5 -> x0, waiting for transfers between devices: 86.9 us -> none
    pallas_call x0 -> x1, Pallas kernels: none -> 80.9 us  [per_device(): pl.pallas_call(kernel, out_shape=(jax.ShapeDtypeStruct((rl, fb), BF16), j...]
    psum x1 -> x0, blocking collectives: 29.6 us -> none  [per_device(): lax.psum((part_hidden, part_upstream), 'narrow')]
    all_to_all x1 -> x0, starting transfers between devices: 11.5 us -> none  [per_device(): lax.all_to_all(ordered, 'wide', split_axis=1, concat_axis=0, tiled=True)]
    dot_general x6 -> x0, matrix products: 10.5 us -> none  [the longest x1 4.43 us: per_device(): lax.dot_general(lax.all_gather(new_b, 'wide', axis=0, tiled=True), right_...]
  transfers between devices with their start and end apart: 5 -> 0, of which waited for: 4 -> 0; matrix products, arithmetic and copies ran while one was open for 3% -> 0% of each run, Pallas kernels for 0% -> 0%
where the time goes in v1:
time: 88.7 us; the launch traced here: 88.6 us
  Pallas kernels  80.9 us (91%)
  local copies, waits for them, and re-layouts  7.02 us (8%)
    pallas_call x1, Pallas kernels, per_device(): pl.pallas_call(kernel, out_shape=(jax.ShapeDtypeStruct((rl, fb), BF16), j...  80.9 us
    unnamed x7, local copies, waits for them, and re-layouts  4.61 us
    pallas_call x1, local copies, waits for them, and re-layouts, per_device(): pl.pallas_call(kernel, out_shape=(jax.ShapeDtypeStruct((rl, fb), BF16), j...  2.42 us

profile of v1, /device:TPU:1, one launch (start us, length us, event | category | flops | bytes accessed | tf_op | source)
XLA Modules:
  0.0 88.6 jit_solution(16033566768354678295)
XLA Ops:
  0.6 0.0 copy-start
  0.6 2.5 %copy.14.cot_h = bf16[1,128,4640]{2,1,0:T(8,128)(2,1)} copy(bf16[1,128,4640]{1,2,0:T(8,128)(2,1)} %param.14) | data formatting | bytes 2375680 | tf_op args[2]
  3.2 0.0 copy-done
  3.2 1.4 %copy.15.res_h = bf16[1024,580]{1,0:T(8,128)(2,1)} copy(bf16[1024,580]{0,1:T(8,128)(2,1)S(1)} %copy-done) | data formatting | bytes 2375680 | tf_op args[9]
  4.6 80.9 %merge_step.1 = (bf16[1024,580]{1,0:T(8,128)(2,1)}, bf16[64,580]{1,0:T(8,128)(2,1)}) custom-call(s32[1,128]{1,0:T(1,128)} %tok_ref.1, s32[64]{0:T(128)} %owner_ref.1, bf16[1,128,1024]{2,1,0:T(8,128)(2,1)} %cache_h.1, bf16[1,128,4640]{2,1,0:T(8,128)(2,1)} %copy.14.cot_h, f32[1,16,1024]{2,1,0:T(8,128)} %ab_h.1, f32[1,16,1024]{2,1,0:T(8,128)} %fb_h.1, ...), custom_call_target="tpu_custom_call" | custom-call | tf_op jit(solution)/shard_map/merge_step/pallas_call | solution.py:566
  85.5 0.0 copy-start.1
  85.5 2.4 %copy.16 = bf16[1024,580]{0,1:T(8,128)(2,1)} copy(bf16[1024,580]{1,0:T(8,128)(2,1)} %get-tuple-element.2) | data formatting | bytes 2375680 | tf_op jit(solution)/shard_map/merge_step/pallas_call | solution.py:566
  87.9 0.0 copy-done.1
  87.9 0.6 copy.18
Async XLA Ops:
  0.6 2.5 %copy-start = (bf16[1024,580]{0,1:T(8,128)(2,1)S(1)}, bf16[1024,580]{0,1:T(8,128)(2,1)}, u32[]{:S(2)}) copy-start(bf16[1024,580]{0,1:T(8,128)(2,1)} %param.21) | copy-start | bytes 3563524
  85.5 2.4 %copy-start.1 = (bf16[64,580]{1,0:T(8,128)(2,1)S(1)}, bf16[64,580]{1,0:T(8,128)(2,1)}, u32[]{:S(2)}) copy-start(bf16[64,580]{1,0:T(8,128)(2,1)} %get-tuple-element.7) | copy-start | bytes 222724

commit v2 on v1

v2 whole, which is shorter than its diff:
```python
import math

import jax
import jax.numpy as jnp
from jax import lax
from jax.experimental import pallas as pl
from jax.experimental.pallas import tpu as pltpu
from jax.sharding import PartitionSpec as P

D = 8192
WORKER_TOKENS = 128
F32 = jnp.float32
BF16 = jnp.bfloat16
MESH = pl.DeviceIdType.MESH

adapter_scale = 4.0
rate = 0.2
beta_one = 0.9
beta_two = 0.999
bias_one = 1.0 - 0.9**20
bias_two = 1.0 - 0.999**20
eps_adam = 1e-08

NZ, NY, NX = 8, 2, 4
LANE = 128


def adam_step(param, first, second, grad):
    first_new = beta_one * first + (1.0 - beta_one) * grad
    second_new = beta_two * second + (1.0 - beta_two) * grad * grad
    update = first_new / bias_one / (jnp.sqrt(second_new / bias_two) + eps_adam)
    return param - rate * update


def split3(v):
    hi = v.astype(BF16)
    rest = v - hi.astype(F32)
    mid = rest.astype(BF16)
    low = (rest - mid.astype(F32)).astype(BF16)
    return jnp.concatenate([hi, mid, low], axis=0)


def sum3(v):
    n = v.shape[0] // 3
    return v[:n] + v[n : 2 * n] + v[2 * n :]


def dot(a, b):
    return lax.dot_general(a, b, (((1,), (0,)), ((), ())), preferred_element_type=F32)


def dot_nt(a, b):
    return lax.dot_general(a, b, (((1,), (1,)), ((), ())), preferred_element_type=F32)


class Gather:
    def __init__(self, ref, lanes, rs, ss, first, pos, n):
        self.ref, self.lanes, self.rs, self.ss, self.n = ref, lanes, rs, ss, n
        self.z, self.y, self.x = pos
        self.first = first
        self.na, self.nb = (NX, NZ) if first == "x" else (NZ, NX)
        self.a, self.b = (self.x, self.z) if first == "x" else (self.z, self.x)

    def index(self, y, a, b):
        z, x = (b, a) if self.first == "x" else (a, b)
        return (z * NY + y) * NX + x

    def view(self, v):
        if self.lanes is None:
            return self.ref.at[v]
        return self.ref.at[v, :, self.lanes]

    def slot_b(self, s, way, y):
        return 3 + ((s - 1) * 2 + (way < 0)) * 2 + y

    def copy(self, v, dest, slot):
        return pltpu.make_async_remote_copy(
            self.view(v), self.view(v), self.ss, self.rs.at[slot], device_id=(dest, self.n), device_id_type=MESH
        )

    def to_b(self, v, way, s, y):
        dest = self.index(self.y, self.a, (self.b + way + self.nb) % self.nb)
        self.copy(v, dest, self.slot_b(s, way, y)).start()

    def arrived(self, slot, count):
        if self.lanes is None:
            r = self.ref.at[pl.ds(0, count)]
        else:
            r = self.ref.at[pl.ds(0, count), :, self.lanes]
        pltpu.make_async_copy(r, r, self.rs.at[slot]).wait()

    def begin(self):
        me = self.index(self.y, self.a, self.b)

        self.copy(me, self.index(1 - self.y, self.a, self.b), 0).start()
        self.along(me, self.y, 1)

    def along(self, v, y, slot):
        def send(d, _):
            self.copy(v, self.index(self.y, (self.a + d) % self.na, self.b), slot).start()
            return 0

        lax.fori_loop(1, self.na, send, 0)
        for way in (1, -1):
            self.to_b(v, way, 1, y)

    def pair(self):
        self.arrived(0, 1)
        self.along(self.index(1 - self.y, self.a, self.b), 1 - self.y, 2)

    def direct(self):
        for slot, y in ((1, self.y), (2, 1 - self.y)):
            self.arrived(slot, self.na - 1)

            def step(d, _):
                v = self.index(y, (self.a + d) % self.na, self.b)
                for way in (1, -1):
                    self.to_b(v, way, 1, y)
                return 0

            lax.fori_loop(1, self.na, step, 0)

    def ring_b(self, s):
        for y in range(NY):
            for way in (1, -1):
                lim = self.nb // 2 - (y == (1 if way == 1 else 0))
                if s <= lim:
                    self.arrived(self.slot_b(s, way, y), self.na)
                    if s < lim:

                        def step(q, _):
                            v = self.index(y, q, (self.b - way * s + self.nb) % self.nb)
                            self.to_b(v, way, s + 1, y)
                            return 0

                        lax.fori_loop(0, self.na, step, 0)

    def sent(self):
        count = self.ref.shape[0] - 1
        if self.lanes is None:
            r = self.ref.at[pl.ds(0, count)]
        else:
            r = self.ref.at[pl.ds(0, count), :, self.lanes]
        pltpu.make_async_copy(r, r, self.ss).wait()


def kernel(
    tok_h, owner_h, cache_h, cot_h, ab_h, fb_h, sb_h, aa_h, fa_h, sa_h, res_h, nxt_h,
    mg, pj,
    tok_ref, owner_ref, cache, cot, ab, fb, sb, aa, fa, sa, res,
    pb, gb, gn, na, s1, bl, st, rv, at, nr, px, pxr, po, rsrc, rrcv, rf, tx, tr, ts, tg, tt,
    in_sem, pb_s, pb_r, gb0_r, gb1_r, gn_r, g_s, t_s, t_r, tw_s, tw_r, rf_r, s1_s, s1_r, s2_s, s2_r, s3_s, s3_r, px_s, px_r, rr_s, rr_r, loc_s,
):
    w = lax.axis_index("wide")
    n = lax.axis_index("narrow")
    x = w % NX
    y = (w // NX) % NY
    z = w // (NX * NY)
    yh = n // 2
    c = n % 2
    nw = NZ * NY * NX
    inverse_root = 1.0 / math.sqrt(D)

    loads = {}
    pairs = (
        ("tok", tok_h, tok_ref), ("ab", ab_h.at[0], ab), ("cache", cache_h.at[0], cache), ("aa", aa_h.at[0], aa), ("cot", cot_h.at[0], cot),
        ("nxt", nxt_h, gn.at[w]), ("fb", fb_h.at[0], fb), ("sb", sb_h.at[0], sb), ("fa", fa_h.at[0], fa),
        ("sa", sa_h.at[0], sa), ("res", res_h, res),
        ("owner", owner_h, owner_ref),
    )
    for i, (name, src, dst) in enumerate(pairs):
        loads[name] = pltpu.make_async_copy(src, dst, in_sem.at[i])
        loads[name].start()

    bar = pltpu.get_barrier_semaphore()

    def sig_w(d, _):
        pl.semaphore_signal(bar, inc=1, device_id=((w + d) % nw, n), device_id_type=MESH)
        return 0

    def sig_n(d, _):
        pl.semaphore_signal(bar, inc=1, device_id=(w, (n + d) % 8), device_id_type=MESH)
        return 0

    lax.fori_loop(1, nw, sig_w, 0)
    lax.fori_loop(1, 8, sig_n, 0)

    loads["tok"].wait()
    oht = (lax.broadcasted_iota(jnp.int32, (128, 128), 0) == tok_ref[...]).astype(F32).astype(BF16)
    loads["ab"].wait()
    loads["cache"].wait()
    hp = sum3(dot_nt(split3(ab[...]), cache[...]))
    ht = sum3(dot(split3(hp), oht))
    loads["aa"].wait()
    loads["cot"].wait()
    ut = sum3(dot(split3(aa[...]), cot[...]))
    qp = sum3(dot_nt(split3(ut), oht))
    pb[n] = jnp.concatenate([ht, qp], axis=0).astype(BF16)

    pl.semaphore_wait(bar, nw - 1 + 7)

    def pb_copy(d):
        return pltpu.make_async_remote_copy(
            pb.at[n], pb.at[n], pb_s, pb_r, device_id=(w, (n + d) % 8), device_id_type=MESH
        )

    def pb_send(d, _):
        pb_copy(d).start()
        return 0

    lax.fori_loop(1, 8, pb_send, 0)

    pos = (z, y, x)
    gath_n = Gather(gn, None, gn_r, g_s.at[0], "z", pos, n)
    gath_0 = Gather(gb, pl.ds(0, 768), gb0_r, g_s.at[1], "z", pos, n)
    gath_1 = Gather(gb, pl.ds(768, 256), gb1_r, g_s.at[2], "x", pos, n)

    loads["nxt"].wait()
    gath_n.begin()
    gath_n.pair()

    r7 = pb.at[pl.ds(0, 7)]
    pltpu.make_async_copy(r7, r7, pb_r).wait()
    total = pb[0].astype(F32)
    for i in range(1, 8):
        total = total + pb[i].astype(F32)
    hid = total[:16] * inverse_root
    qsum = total[16:]

    grad_b = adapter_scale * inverse_root / WORKER_TOKENS * sum3(dot(split3(qsum), cache[...]))
    loads["fb"].wait()
    loads["sb"].wait()
    gb[w] = adam_step(ab[...], fb[...], sb[...], grad_b).astype(BF16)
    gath_0.begin()
    gath_1.begin()

    hs = split3(hid)
    loads["fa"].wait()
    loads["sa"].wait()
    cols = cot.shape[0]
    na[:, 4608:] = jnp.zeros((16, 128), F32)
    edges = (0, 1152, 2304, 3456, cols)
    for lo, hi in zip(edges[:-1], edges[1:]):
        grad_a = adapter_scale / WORKER_TOKENS * sum3(dot_nt(hs, cot[lo:hi, :]))
        na[:, lo:hi] = adam_step(aa[:, lo:hi], fa[:, lo:hi], sa[:, lo:hi], grad_a)
    fbk = cols // 8
    for k in range(8):
        base = fbk * k // LANE * LANE
        shift = fbk * k - base
        win = na[:, base : base + 768]
        if shift:
            win = pltpu.roll(win, 768 - shift, 1)
        blk = win[:, :640].astype(BF16)
        for t in range(5):
            s1[t, k] = blk[:, t * LANE : (t + 1) * LANE]

    own8 = pl.ds(n * 8, 8)
    holders = ((0, 0), (1, 2), (2, 4), (3, 6), (4, 1), (4, 5))

    def s1_copy(i):
        t, dest = holders[i]
        return pltpu.make_async_remote_copy(
            s1.at[t], bl.at[own8], s1_s.at[i], s1_r, device_id=(w, dest), device_id_type=MESH
        )

    for i, (t, dest) in enumerate(holders):

        @pl.when(n != dest)
        def _():
            s1_copy(i).start()

        @pl.when(n == dest)
        def _():
            bl[own8] = s1[t]

    gath_1.pair()
    gath_0.pair()
    gath_n.direct()
    gath_1.direct()
    gath_n.ring_b(1)

    even = c == 0
    holds = jnp.logical_or(even, jnp.logical_or(n == 1, n == 5))
    y4 = n // 4
    gets = jnp.logical_or(even, jnp.logical_or(jnp.logical_and(n == 1, y == 0), jnp.logical_and(n == 5, y == 1)))
    tile = jnp.where(even, yh, 4)

    @pl.when(holds)
    def _():
        r = bl.at[pl.ds(0, 56)]
        pltpu.make_async_copy(r, r, s1_r).wait()

        loads["owner"].wait()

        def pick(j, _):
            st[j] = bl[owner_ref[j]]
            return 0

        lax.fori_loop(0, nw, pick, 0)

    def s2_copy(j):
        return pltpu.make_async_remote_copy(
            st.at[j], rv.at[w], s2_s, s2_r, device_id=(j, n), device_id_type=MESH
        )

    @pl.when(even)
    def _():
        def send(d, _):
            s2_copy((w + d) % nw).start()
            return 0

        lax.fori_loop(1, nw, send, 0)

    @pl.when(jnp.logical_and(holds, jnp.logical_not(even)))
    def _():
        def send(d, _):
            j = (w + d) % nw

            @pl.when((j // NX) % NY == y4)
            def _():
                s2_copy(j).start()

            return 0

        lax.fori_loop(1, nw, send, 0)

    @pl.when(gets)
    def _():
        own = pltpu.make_async_copy(st.at[w], rv.at[w], loc_s)
        own.start()
        own.wait()

    gath_0.direct()
    gath_n.ring_b(2)
    for i in range(8):
        rows = gn[pl.ds(i * 8, 8)].astype(F32).reshape(64, gn.shape[2]).astype(BF16)
        nr[i // 2, i % 2] = rows

    loads["res"].wait()
    partner = yh * 2 + 1 - c
    px[...] = dot_nt(nr[:, 1 - c].reshape(256, nr.shape[3]), res[...]).astype(BF16)
    xcopy = pltpu.make_async_remote_copy(px, pxr, px_s, px_r, device_id=(w, partner), device_id_type=MESH)
    xcopy.start()

    for h in range(4):
        tx[h] = dot_nt(gb[w], nr[h].reshape(128, nr.shape[3])).astype(BF16)
    tr[n] = tx[yh]

    def t_copy(d):
        dest = (n + d) % 8
        return pltpu.make_async_remote_copy(
            tx.at[dest // 2], tr.at[n], t_s.at[d - 1], t_r, device_id=(w, dest), device_id_type=MESH
        )

    for d in range(1, 8):
        t_copy(d).start()

    po[...] = dot_nt(nr[:, c].reshape(256, nr.shape[3]), res[...]).reshape(po.shape)
    gath_1.ring_b(1)
    xcopy.wait_recv()
    for h in range(4):
        po[h] = po[h] + pxr[h * 64 : (h + 1) * 64].astype(F32)
    up, down, far = (yh + 1) % 4, (yh + 3) % 4, (yh + 2) % 4
    rsrc[2] = po[far].astype(BF16)

    def far_copy(i, h):
        half = pl.ds(32 * i, 32)
        return pltpu.make_async_remote_copy(
            rsrc.at[2, half], rf.at[i], rr_s.at[2 + i], rf_r.at[i], device_id=(w, h * 2 + c), device_id_type=MESH
        )

    def near_copy(i, h):
        return pltpu.make_async_remote_copy(
            rsrc.at[i], rrcv.at[i], rr_s.at[i], rr_r, device_id=(w, h * 2 + c), device_id_type=MESH
        )

    far_copy(0, up).start()
    far_copy(1, down).start()

    gath_0.ring_b(1)
    pltpu.make_async_copy(tr.at[pl.ds(0, 7)], tr.at[pl.ds(0, 7)], t_r).wait()
    tsum = tr[0].astype(F32)
    for i in range(1, 8):
        tsum = tsum + tr[i].astype(F32)
    ts[...] = tsum.astype(BF16)
    tg[w] = ts[...]

    def tw_send(d, _):
        pltpu.make_async_remote_copy(
            ts, tg.at[w], tw_s, tw_r, device_id=((w + d) % nw, n), device_id_type=MESH
        ).start()
        return 0

    lax.fori_loop(1, nw, tw_send, 0)

    far_copy(0, up).wait_recv()
    far_copy(1, down).wait_recv()
    toward = po[up]
    rsrc[0] = jnp.concatenate([toward[:32] + rf[0].astype(F32), toward[32:]], axis=0).astype(BF16)
    near_copy(0, up).start()
    toward = po[down]
    rsrc[1] = jnp.concatenate([toward[:32], toward[32:] + rf[1].astype(F32)], axis=0).astype(BF16)
    near_copy(1, down).start()

    @pl.when(gets)
    def _():
        r = rv.at[pl.ds(0, nw - 1)]
        pltpu.make_async_copy(r, r, s2_r).wait()
        right = rv[...].reshape(nw * 16, LANE).T

        @pl.when(even)
        def _():
            at[pl.ds(pl.multiple_of(yh * LANE, LANE), LANE), :] = right

        @pl.when(jnp.logical_not(even))
        def _():
            at[4 * LANE :, :] = right[: at.shape[0] - 4 * LANE]

    def piece(t, half):
        if isinstance(t, int) and t == 4:
            return at.at[pl.ds(t * LANE + half * 48, 48 - half * 16)]
        return at.at[pl.ds(pl.multiple_of(t * LANE + half * 64, 64), 64)]


    def s3(t, half, slot, sem, dest):
        return pltpu.make_async_remote_copy(
            piece(t, half), piece(t, half), s3_s.at[sem], s3_r.at[slot], device_id=(w, dest), device_id_type=MESH
        )

    d4 = (yh - 2 * y + 4) % 4
    even_sends = (
        (yh, 0, 2, 0, up * 2), (yh, 1, 5, 1, down * 2), (yh, 1, 3, 2, up * 2), (yh, 0, 4, 3, down * 2),
        (yh, 0, 0, 4, partner), (yh, 1, 1, 5, partner),
    )
    src_sends = (
        (4, 0, 8, 0, up * 2 + 1), (4, 1, 9, 1, down * 2 + 1), (4, 1, 9, 2, up * 2 + 1), (4, 0, 8, 3, down * 2 + 1),
        (4, 0, 8, 4, partner), (4, 1, 9, 5, partner),
    )

    @pl.when(even)
    def _():
        for args in even_sends:
            s3(*args).start()

    @pl.when(jnp.logical_and(c == 1, d4 == 0))
    def _():
        for args in src_sends:
            s3(*args).start()

    gath_1.ring_b(2)
    gath_0.ring_b(2)
    gath_1.ring_b(3)
    @pl.when(even)
    def _():
        s3(down, 0, 2, 0, partner).wait_recv()
        s3(down, 0, 6, 6, up * 2).start()
        s3(down, 0, 2, 7, partner).start()
        s3(up, 1, 5, 0, partner).wait_recv()
        s3(up, 1, 7, 8, down * 2).start()
        s3(up, 1, 5, 9, partner).start()

    @pl.when(jnp.logical_and(c == 1, d4 == 1))
    def _():
        s3(4, 0, 8, 0, partner).wait_recv()
        s3(4, 0, 8, 0, up * 2 + 1).start()
        s3(4, 0, 8, 1, partner).start()
        s3(4, 1, 9, 0, partner).wait_recv()
        s3(4, 1, 9, 2, partner).start()

    @pl.when(jnp.logical_and(c == 1, d4 == 3))
    def _():
        s3(4, 1, 9, 0, partner).wait_recv()
        s3(4, 1, 9, 0, down * 2 + 1).start()
        s3(4, 1, 9, 1, partner).start()
        s3(4, 0, 8, 0, partner).wait_recv()
        s3(4, 0, 8, 2, partner).start()

    gath_1.ring_b(4)
    @pl.when(even)
    def _():
        s3(down, 1, 3, 0, partner).wait_recv()
        s3(down, 1, 3, 10, partner).start()
        s3(up, 0, 4, 0, partner).wait_recv()
        s3(up, 0, 4, 11, partner).start()

    @pl.when(even)
    def _():
        s3(far, 0, 6, 0, partner).wait_recv()
        s3(far, 0, 6, 12, partner).start()
        s3(far, 1, 7, 0, partner).wait_recv()
        s3(far, 1, 7, 13, partner).start()
        s3(4, 0, 8, 0, partner).wait_recv()
        s3(4, 1, 9, 0, partner).wait_recv()

    @pl.when(jnp.logical_and(c == 1, d4 == 2))
    def _():
        s3(4, 0, 8, 0, partner).wait_recv()
        s3(4, 0, 8, 0, partner).start()
        s3(4, 1, 9, 0, partner).wait_recv()
        s3(4, 1, 9, 1, partner).start()

    @pl.when(c == 1)
    def _():
        for t, half, slot in (
            (yh, 0, 0), (yh, 1, 1), (down, 0, 2), (down, 1, 3), (up, 0, 4), (up, 1, 5), (far, 0, 6), (far, 1, 7),
        ):
            s3(t, half, slot, 0, partner).wait_recv()

    fbw = res.shape[0]
    for t in range(res.shape[1] // 256):
        part = slice(t * 256, (t + 1) * 256)
        delta = dot(at[...], gb[:, :, part].reshape(nw * 16, 256))
        mg[:, part] = (res[:, part].astype(F32) + adapter_scale / nw * delta[:fbw]).astype(BF16)

    rt = tg.at[pl.ds(0, nw - 1)]
    pltpu.make_async_copy(rt, rt, tw_r).wait()
    term = dot(at[...], tg[...].reshape(nw * 16, LANE))
    tt[...] = term.T.reshape(tt.shape)
    pltpu.make_async_copy(rrcv, rrcv, rr_r).wait()
    acc = po[yh] + rrcv[0].astype(F32) + rrcv[1].astype(F32)
    acc = acc + adapter_scale / nw * tt[c][:, :fbw]
    pj[...] = (acc * inverse_root).astype(BF16)

    @pl.when(jnp.logical_not(holds))
    def _():
        loads["owner"].wait()

    pltpu.make_async_copy(r7, r7, pb_s).wait()
    gath_n.sent()
    gath_0.sent()
    gath_1.sent()
    pltpu.make_async_copy(rt, rt, tw_s).wait()
    for d in range(1, 8):
        t_copy(d).wait_send()
    for i, (t, dest) in enumerate(holders):

        @pl.when(n != dest)
        def _():
            s1_copy(i).wait_send()

    @pl.when(even)
    def _():
        r = st.at[pl.ds(0, nw - 1)]
        pltpu.make_async_copy(r, r, s2_s).wait()
        for i in range(14):
            s3(0, 0, 0, i, partner).wait_send()

    @pl.when(jnp.logical_and(holds, jnp.logical_not(even)))
    def _():
        @pl.when(gets)
        def _():
            r = st.at[pl.ds(0, nw // 2 - 1)]
            pltpu.make_async_copy(r, r, s2_s).wait()

        @pl.when(jnp.logical_not(gets))
        def _():
            r = st.at[pl.ds(0, nw // 2)]
            pltpu.make_async_copy(r, r, s2_s).wait()

    for d, halves in ((0, (0, 1, 1, 0, 0, 1)), (1, (0, 0, 1)), (2, (0, 1)), (3, (1, 1, 0))):

        @pl.when(jnp.logical_and(c == 1, d4 == d))
        def _():
            for i, half in enumerate(halves):
                s3(4, half, 0, i, partner).wait_send()

    xcopy.wait_send()
    far_copy(0, up).wait_send()
    far_copy(1, down).wait_send()
    near_copy(0, up).wait_send()
    near_copy(1, down).wait_send()


def per_device(
    activation_cache, token_ids, cotangent, adapter_b, first_b, second_b, adapter_a, first_a, second_a, resident,
    block_owner, next_rows,
):
    dl = activation_cache.shape[2]
    cl = cotangent.shape[2]
    rl, fb = resident.shape
    nw = NZ * NY * NX
    anyspec = pl.BlockSpec(memory_space=pl.ANY)
    dma = pltpu.SemaphoreType.DMA
    vm = pltpu.VMEM
    scratch = [
        vm((1, 128), jnp.int32), pltpu.SMEM((nw,), jnp.int32),
        vm((128, dl), BF16), vm((cl, 128), BF16), vm((16, dl), F32), vm((16, dl), F32), vm((16, dl), F32),
        vm((16, cl), F32), vm((16, cl), F32), vm((16, cl), F32), vm((fb, rl), BF16),
        vm((8, 32, 128), BF16),
        vm((nw, 16, dl), BF16),
        vm((nw, 8, dl), BF16),
        vm((16, 4736), F32),
        vm((5, 8, 16, LANE), BF16),
        vm((nw, 16, LANE), BF16),
        vm((nw, 16, LANE), BF16),
        vm((nw, 16, LANE), BF16),
        vm((4 * LANE + 80, nw * 16), BF16),
        vm((4, 2, 64, dl), BF16),
        vm((256, fb), BF16), vm((256, fb), BF16),
        vm((4, 64, fb), F32),
        vm((3, 64, fb), BF16), vm((2, 64, fb), BF16),
        vm((2, 32, fb), BF16),
        vm((4, 16, LANE), BF16), vm((8, 16, LANE), BF16), vm((16, LANE), BF16), vm((nw, 16, LANE), BF16),
        vm((2, 64, 4 * LANE + 80), F32),
        dma((12,)), dma(()), dma(()),
        dma((11,)), dma((19,)), dma((11,)), dma((3,)),
        dma((7,)), dma(()), dma(()), dma(()), dma((2,)),
        dma((6,)), dma(()), dma(()), dma(()),
        dma((14,)), dma((10,)),
        dma(()), dma(()), dma((4,)), dma(()), dma(()),
    ]
    merged, projected = pl.pallas_call(
        kernel,
        out_shape=(pltpu.VMEM((fb, rl), BF16), pltpu.VMEM((64, fb), BF16)),
        in_specs=[anyspec] * 12,
        out_specs=(pl.BlockSpec(memory_space=pltpu.VMEM),) * 2,
        scratch_shapes=scratch,
        compiler_params=pltpu.CompilerParams(collective_id=0, has_side_effects=True, vmem_limit_bytes=60 * 1024 * 1024),
        name="merge_step",
    )(
        token_ids, block_owner, activation_cache, jnp.swapaxes(cotangent, 1, 2), adapter_b, first_b, second_b, adapter_a,
        first_a, second_a, resident.T, next_rows,
    )
    return merged.T, projected


def solution(mesh):
    return jax.shard_map(
        per_device,
        mesh=mesh,
        in_specs=(
            P("wide", None, "narrow"),
            P("wide", None),
            P("wide", None, "narrow"),
            P("wide", None, "narrow"),
            P("wide", None, "narrow"),
            P("wide", None, "narrow"),
            P("wide", None, "narrow"),
            P("wide", None, "narrow"),
            P("wide", None, "narrow"),
            P("narrow", "wide"),
            P(),
            P("wide", "narrow"),
        ),
        out_specs=(P("narrow", "wide"), P("narrow", "wide")),
        check_vma=False,
    )
```

time: 88.7 us -> 73.3 us (0.83)
  Pallas kernels: 80.9 us -> 70.9 us
  local copies, waits for them, and re-layouts: 7.02 us -> 1.66 us
    pallas_call x1, Pallas kernels: 80.9 us -> 70.9 us  [per_device(): pl.pallas_call(kernel, out_shape=(pltpu.VMEM((fb, rl), BF16), pltpu.VMEM(...]
    unnamed x7 -> x2, local copies, waits for them, and re-layouts: 4.61 us -> 1.66 us
    pallas_call x1 -> x0, local copies, waits for them, and re-layouts: 2.42 us -> none  [per_device(): pl.pallas_call(kernel, out_shape=(jax.ShapeDtypeStruct((rl, fb), BF16), j...]
where the time goes in v2:
time: 73.3 us; the launch traced here: 73.2 us
  Pallas kernels  70.9 us (97%)
  local copies, waits for them, and re-layouts  1.66 us (2%)
    pallas_call x1, Pallas kernels, per_device(): pl.pallas_call(kernel, out_shape=(pltpu.VMEM((fb, rl), BF16), pltpu.VMEM(...  70.9 us
    unnamed x2, local copies, waits for them, and re-layouts  1.66 us

profile of v2, /device:TPU:1, one launch (start us, length us, event | category | flops | bytes accessed | tf_op | source)
XLA Modules:
  0.0 73.2 jit_solution(11563505967946415013)
XLA Ops:
  0.6 70.9 %merge_step.1 = (bf16[580,1024]{1,0:T(8,128)(2,1)S(1)}, bf16[64,580]{1,0:T(8,128)(2,1)S(1)}) custom-call(s32[1,128]{1,0:T(1,128)} %tok_h.1, s32[64]{0:T(128)} %owner_h.1, bf16[1,128,1024]{2,1,0:T(8,128)(2,1)} %cache_h.1, bf16[1,4640,128]{2,1,0:T(8,128)(2,1)} %bitcast.5, f32[1,16,1024]{2,1,0:T(8,128)} %ab_h.1, f32[1,16,1024]{2,1,0:T(8,128)} %fb_h.1, ...), custom_call_target="tpu_custom_call" | custom-call | tf_op jit(solution)/shard_map/merge_step/pallas_call | solution.py:612
  71.5 1.0 %copy.16 = bf16[1024,580]{0,1:T(8,128)(2,1)} copy(bf16[1024,580]{0,1:T(8,128)(2,1)S(1)} %bitcast.3) | data formatting | bytes 2375680
  72.5 0.6 copy.17

commit v3 on v2

--- a/solution.py
+++ b/solution.py
@@ -71,7 +71,7 @@
         return self.ref.at[v, :, self.lanes]
 
     def slot_b(self, s, way, y):
-        return 3 + ((s - 1) * 2 + (way < 0)) * 2 + y
+        return 1 + self.na // 2 + ((s - 1) * 2 + (way < 0)) * 2 + y
 
     def copy(self, v, dest, slot):
         return pltpu.make_async_remote_copy(
@@ -93,32 +93,29 @@
         me = self.index(self.y, self.a, self.b)
 
         self.copy(me, self.index(1 - self.y, self.a, self.b), 0).start()
-        self.along(me, self.y, 1)
-
-    def along(self, v, y, slot):
-        def send(d, _):
-            self.copy(v, self.index(self.y, (self.a + d) % self.na, self.b), slot).start()
-            return 0
-
-        lax.fori_loop(1, self.na, send, 0)
+        self.along(me, self.y)
+
+    def steps(self, dist):
+        return (dist,) if dist == self.na // 2 else (dist, -dist)
+
+    def along(self, v, y):
         for way in (1, -1):
             self.to_b(v, way, 1, y)
+        for dist in range(1, self.na // 2 + 1):
+            for d in self.steps(dist):
+                self.copy(v, self.index(self.y, (self.a + d + self.na) % self.na, self.b), dist).start()
 
     def pair(self):
         self.arrived(0, 1)
-        self.along(self.index(1 - self.y, self.a, self.b), 1 - self.y, 2)
-
-    def direct(self):
-        for slot, y in ((1, self.y), (2, 1 - self.y)):
-            self.arrived(slot, self.na - 1)
-
-            def step(d, _):
-                v = self.index(y, (self.a + d) % self.na, self.b)
+        self.along(self.index(1 - self.y, self.a, self.b), 1 - self.y)
+
+    def direct(self, dist):
+        self.arrived(dist, 2 * len(self.steps(dist)))
+        for y in range(NY):
+            for d in self.steps(dist):
+                v = self.index(y, (self.a + d + self.na) % self.na, self.b)
                 for way in (1, -1):
                     self.to_b(v, way, 1, y)
-                return 0
-
-            lax.fori_loop(1, self.na, step, 0)
 
     def ring_b(self, s):
         for y in range(NY):
@@ -149,7 +146,7 @@
     mg, pj,
     tok_ref, owner_ref, cache, cot, ab, fb, sb, aa, fa, sa, res,
     pb, gb, gn, na, s1, bl, st, rv, at, nr, px, pxr, po, rsrc, rrcv, rf, tx, tr, ts, tg, tt,
-    in_sem, pb_s, pb_r, gb0_r, gb1_r, gn_r, g_s, t_s, t_r, tw_s, tw_r, rf_r, s1_s, s1_r, s2_s, s2_r, s3_s, s3_r, px_s, px_r, rr_s, rr_r, loc_s,
+    in_sem, pb_s, pb_r, gb0_r, gb1_r, gn_r, g_s, t_s, t_r, tw_s, tw_r, te_s, te_r, rf_r, s1_s, s1_r, s2_s, s2_r, s3_s, s3_r, px_s, px_r, rr_s, rr_r, loc_s,
 ):
     w = lax.axis_index("wide")
     n = lax.axis_index("narrow")
@@ -211,9 +208,9 @@
     lax.fori_loop(1, 8, pb_send, 0)
 
     pos = (z, y, x)
-    gath_n = Gather(gn, None, gn_r, g_s.at[0], "z", pos, n)
-    gath_0 = Gather(gb, pl.ds(0, 768), gb0_r, g_s.at[1], "z", pos, n)
-    gath_1 = Gather(gb, pl.ds(768, 256), gb1_r, g_s.at[2], "x", pos, n)
+    gath_n = Gather(gn, None, gn_r, g_s.at[2], "z", pos, n)
+    gath_0 = Gather(gb, pl.ds(0, 768), gb0_r, g_s.at[0], "z", pos, n)
+    gath_1 = Gather(gb, pl.ds(768, 256), gb1_r, g_s.at[1], "x", pos, n)
 
     loads["nxt"].wait()
     gath_n.begin()
@@ -231,8 +228,6 @@
     loads["fb"].wait()
     loads["sb"].wait()
     gb[w] = adam_step(ab[...], fb[...], sb[...], grad_b).astype(BF16)
-    gath_0.begin()
-    gath_1.begin()
 
     hs = split3(hid)
     loads["fa"].wait()
@@ -273,11 +268,12 @@
         def _():
             bl[own8] = s1[t]
 
-    gath_1.pair()
-    gath_0.pair()
-    gath_n.direct()
-    gath_1.direct()
-    gath_n.ring_b(1)
+    gath_n.direct(1)
+    gath_n.direct(2)
+    gath_n.direct(3)
+    gath_n.direct(4)
+    gath_0.begin()
+    gath_1.begin()
 
     even = c == 0
     holds = jnp.logical_or(even, jnp.logical_or(n == 1, n == 5))
@@ -330,7 +326,9 @@
         own.start()
         own.wait()
 
-    gath_0.direct()
+    gath_n.ring_b(1)
+    gath_1.pair()
+    gath_0.pair()
     gath_n.ring_b(2)
     for i in range(8):
         rows = gn[pl.ds(i * 8, 8)].astype(F32).reshape(64, gn.shape[2]).astype(BF16)
@@ -344,23 +342,30 @@
 
     for h in range(4):
         tx[h] = dot_nt(gb[w], nr[h].reshape(128, nr.shape[3])).astype(BF16)
-    tr[n] = tx[yh]
+    leads = c == y
+
+    @pl.when(leads)
+    def _():
+        tr[n] = tx[yh]
 
     def t_copy(d):
-        dest = (n + d) % 8
-        return pltpu.make_async_remote_copy(
-            tx.at[dest // 2], tr.at[n], t_s.at[d - 1], t_r, device_id=(w, dest), device_id_type=MESH
-        )
-
-    for d in range(1, 8):
+        h = (yh + d) % 4
+        return pltpu.make_async_remote_copy(
+            tx.at[h], tr.at[n], t_s.at[d], t_r, device_id=(w, h * 2 + y), device_id_type=MESH
+        )
+
+    for d in (2, 1, 3):
         t_copy(d).start()
 
+    @pl.when(jnp.logical_not(leads))
+    def _():
+        t_copy(0).start()
+
+    up, down, far = (yh + 1) % 4, (yh + 3) % 4, (yh + 2) % 4
     po[...] = dot_nt(nr[:, c].reshape(256, nr.shape[3]), res[...]).reshape(po.shape)
-    gath_1.ring_b(1)
     xcopy.wait_recv()
     for h in range(4):
         po[h] = po[h] + pxr[h * 64 : (h + 1) * 64].astype(F32)
-    up, down, far = (yh + 1) % 4, (yh + 3) % 4, (yh + 2) % 4
     rsrc[2] = po[far].astype(BF16)
 
     def far_copy(i, h):
@@ -376,32 +381,10 @@
 
     far_copy(0, up).start()
     far_copy(1, down).start()
-
-    gath_0.ring_b(1)
-    pltpu.make_async_copy(tr.at[pl.ds(0, 7)], tr.at[pl.ds(0, 7)], t_r).wait()
-    tsum = tr[0].astype(F32)
-    for i in range(1, 8):
-        tsum = tsum + tr[i].astype(F32)
-    ts[...] = tsum.astype(BF16)
-    tg[w] = ts[...]
-
-    def tw_send(d, _):
-        pltpu.make_async_remote_copy(
-            ts, tg.at[w], tw_s, tw_r, device_id=((w + d) % nw, n), device_id_type=MESH
-        ).start()
-        return 0
-
-    lax.fori_loop(1, nw, tw_send, 0)
-
-    far_copy(0, up).wait_recv()
-    far_copy(1, down).wait_recv()
-    toward = po[up]
-    rsrc[0] = jnp.concatenate([toward[:32] + rf[0].astype(F32), toward[32:]], axis=0).astype(BF16)
-    near_copy(0, up).start()
-    toward = po[down]
-    rsrc[1] = jnp.concatenate([toward[:32], toward[32:] + rf[1].astype(F32)], axis=0).astype(BF16)
-    near_copy(1, down).start()
-
+    gath_0.direct(1)
+    gath_0.direct(2)
+    gath_1.direct(1)
+    gath_1.direct(2)
     @pl.when(gets)
     def _():
         r = rv.at[pl.ds(0, nw - 1)]
@@ -420,7 +403,6 @@
         if isinstance(t, int) and t == 4:
             return at.at[pl.ds(t * LANE + half * 48, 48 - half * 16)]
         return at.at[pl.ds(pl.multiple_of(t * LANE + half * 64, 64), 64)]
-
 
     def s3(t, half, slot, sem, dest):
         return pltpu.make_async_remote_copy(
@@ -447,9 +429,27 @@
         for args in src_sends:
             s3(*args).start()
 
-    gath_1.ring_b(2)
-    gath_0.ring_b(2)
-    gath_1.ring_b(3)
+    gath_0.direct(3)
+    gath_0.direct(4)
+    gath_1.ring_b(1)
+
+    @pl.when(leads)
+    def _():
+        pltpu.make_async_copy(tr.at[pl.ds(0, 7)], tr.at[pl.ds(0, 7)], t_r).wait()
+        tsum = tr[0].astype(F32)
+        for i in range(1, 8):
+            tsum = tsum + tr[i].astype(F32)
+        ts[...] = tsum.astype(BF16)
+        tg[w] = ts[...]
+
+        def tw_send(d, _):
+            pltpu.make_async_remote_copy(
+                ts, tg.at[w], tw_s, tw_r, device_id=((w + d) % nw, n), device_id_type=MESH
+            ).start()
+            return 0
+
+        lax.fori_loop(1, nw, tw_send, 0)
+
     @pl.when(even)
     def _():
         s3(down, 0, 2, 0, partner).wait_recv()
@@ -475,7 +475,18 @@
         s3(4, 0, 8, 0, partner).wait_recv()
         s3(4, 0, 8, 2, partner).start()
 
-    gath_1.ring_b(4)
+    gath_0.ring_b(1)
+    gath_1.ring_b(2)
+    far_copy(0, up).wait_recv()
+    far_copy(1, down).wait_recv()
+    toward = po[up]
+    rsrc[0] = jnp.concatenate([toward[:32] + rf[0].astype(F32), toward[32:]], axis=0).astype(BF16)
+    near_copy(0, up).start()
+    toward = po[down]
+    rsrc[1] = jnp.concatenate([toward[:32], toward[32:] + rf[1].astype(F32)], axis=0).astype(BF16)
+    near_copy(1, down).start()
+
+    gath_1.ring_b(3)
     @pl.when(even)
     def _():
         s3(down, 1, 3, 0, partner).wait_recv()
@@ -499,6 +510,28 @@
         s3(4, 1, 9, 0, partner).wait_recv()
         s3(4, 1, 9, 1, partner).start()
 
+    def te_copy(i):
+        span = pl.ds((i * NY + c) * NX, NX)
+        return pltpu.make_async_remote_copy(
+            tg.at[span], tg.at[span], te_s, te_r, device_id=(w, partner), device_id_type=MESH
+        )
+
+    half_tg = tg.at[pl.ds(0, nw // 2)]
+
+    @pl.when(leads)
+    def _():
+        r = tg.at[pl.ds(0, nw // 2 - 1)]
+        pltpu.make_async_copy(r, r, tw_r).wait()
+
+    @pl.when(jnp.logical_not(leads))
+    def _():
+        pltpu.make_async_copy(half_tg, half_tg, tw_r).wait()
+
+    for i in range(NZ):
+        te_copy(i).start()
+
+    gath_1.ring_b(4)
+    gath_0.ring_b(2)
     @pl.when(c == 1)
     def _():
         for t, half, slot in (
@@ -512,8 +545,7 @@
         delta = dot(at[...], gb[:, :, part].reshape(nw * 16, 256))
         mg[:, part] = (res[:, part].astype(F32) + adapter_scale / nw * delta[:fbw]).astype(BF16)
 
-    rt = tg.at[pl.ds(0, nw - 1)]
-    pltpu.make_async_copy(rt, rt, tw_r).wait()
+    pltpu.make_async_copy(half_tg, half_tg, te_r).wait()
     term = dot(at[...], tg[...].reshape(nw * 16, LANE))
     tt[...] = term.T.reshape(tt.shape)
     pltpu.make_async_copy(rrcv, rrcv, rr_r).wait()
@@ -529,8 +561,18 @@
     gath_n.sent()
     gath_0.sent()
     gath_1.sent()
-    pltpu.make_async_copy(rt, rt, tw_s).wait()
-    for d in range(1, 8):
+    pltpu.make_async_copy(half_tg, half_tg, te_s).wait()
+
+    @pl.when(leads)
+    def _():
+        r = tg.at[pl.ds(0, nw - 1)]
+        pltpu.make_async_copy(r, r, tw_s).wait()
+
+    @pl.when(jnp.logical_not(leads))
+    def _():
+        t_copy(0).wait_send()
+
+    for d in (1, 2, 3):
         t_copy(d).wait_send()
     for i, (t, dest) in enumerate(holders):
 
@@ -603,8 +645,8 @@
         vm((4, 16, LANE), BF16), vm((8, 16, LANE), BF16), vm((16, LANE), BF16), vm((nw, 16, LANE), BF16),
         vm((2, 64, 4 * LANE + 80), F32),
         dma((12,)), dma(()), dma(()),
-        dma((11,)), dma((19,)), dma((11,)), dma((3,)),
-        dma((7,)), dma(()), dma(()), dma(()), dma((2,)),
+        dma((13,)), dma((19,)), dma((13,)), dma((3,)),
+        dma((4,)), dma(()), dma(()), dma(()), dma(()), dma(()), dma((2,)),
         dma((6,)), dma(()), dma(()), dma(()),
         dma((14,)), dma((10,)),
         dma(()), dma(()), dma((4,)), dma(()), dma(()),

time: 73.3 us -> 66.2 us (0.903)
  Pallas kernels: 70.9 us -> 63.8 us
    pallas_call x1, Pallas kernels: 70.9 us -> 63.8 us  [per_device(): pl.pallas_call(kernel, out_shape=(pltpu.VMEM((fb, rl), BF16), pltpu.VMEM(...]
where the time goes in v3:
time: 66.2 us; the launch traced here: 66.1 us
  Pallas kernels  63.8 us (96%)
  local copies, waits for them, and re-layouts  1.66 us (3%)
    pallas_call x1, Pallas kernels, per_device(): pl.pallas_call(kernel, out_shape=(pltpu.VMEM((fb, rl), BF16), pltpu.VMEM(...  63.8 us
    unnamed x2, local copies, waits for them, and re-layouts  1.66 us

profile of v3, /device:TPU:1, one launch (start us, length us, event | category | flops | bytes accessed | tf_op | source)
XLA Modules:
  0.0 66.1 jit_solution(8956341686132298859)
XLA Ops:
  0.6 63.8 %merge_step.1 = (bf16[580,1024]{1,0:T(8,128)(2,1)S(1)}, bf16[64,580]{1,0:T(8,128)(2,1)S(1)}) custom-call(s32[1,128]{1,0:T(1,128)} %tok_h.1, s32[64]{0:T(128)} %owner_h.1, bf16[1,128,1024]{2,1,0:T(8,128)(2,1)} %cache_h.1, bf16[1,4640,128]{2,1,0:T(8,128)(2,1)} %bitcast.5, f32[1,16,1024]{2,1,0:T(8,128)} %ab_h.1, f32[1,16,1024]{2,1,0:T(8,128)} %fb_h.1, ...), custom_call_target="tpu_custom_call" | custom-call | tf_op jit(solution)/shard_map/merge_step/pallas_call | solution.py:654
  64.5 1.0 %copy.16 = bf16[1024,580]{0,1:T(8,128)(2,1)} copy(bf16[1024,580]{0,1:T(8,128)(2,1)S(1)} %bitcast.3) | data formatting | bytes 2375680
  65.5 0.6 copy.17

commit v4 on v3

--- a/solution.py
+++ b/solution.py
@@ -362,29 +362,6 @@
         t_copy(0).start()
 
     up, down, far = (yh + 1) % 4, (yh + 3) % 4, (yh + 2) % 4
-    po[...] = dot_nt(nr[:, c].reshape(256, nr.shape[3]), res[...]).reshape(po.shape)
-    xcopy.wait_recv()
-    for h in range(4):
-        po[h] = po[h] + pxr[h * 64 : (h + 1) * 64].astype(F32)
-    rsrc[2] = po[far].astype(BF16)
-
-    def far_copy(i, h):
-        half = pl.ds(32 * i, 32)
-        return pltpu.make_async_remote_copy(
-            rsrc.at[2, half], rf.at[i], rr_s.at[2 + i], rf_r.at[i], device_id=(w, h * 2 + c), device_id_type=MESH
-        )
-
-    def near_copy(i, h):
-        return pltpu.make_async_remote_copy(
-            rsrc.at[i], rrcv.at[i], rr_s.at[i], rr_r, device_id=(w, h * 2 + c), device_id_type=MESH
-        )
-
-    far_copy(0, up).start()
-    far_copy(1, down).start()
-    gath_0.direct(1)
-    gath_0.direct(2)
-    gath_1.direct(1)
-    gath_1.direct(2)
     @pl.when(gets)
     def _():
         r = rv.at[pl.ds(0, nw - 1)]
@@ -429,6 +406,29 @@
         for args in src_sends:
             s3(*args).start()
 
+    po[...] = dot_nt(nr[:, c].reshape(256, nr.shape[3]), res[...]).reshape(po.shape)
+    xcopy.wait_recv()
+    for h in range(4):
+        po[h] = po[h] + pxr[h * 64 : (h + 1) * 64].astype(F32)
+    rsrc[2] = po[far].astype(BF16)
+
+    def far_copy(i, h):
+        half = pl.ds(32 * i, 32)
+        return pltpu.make_async_remote_copy(
+            rsrc.at[2, half], rf.at[i], rr_s.at[2 + i], rf_r.at[i], device_id=(w, h * 2 + c), device_id_type=MESH
+        )
+
+    def near_copy(i, h):
+        return pltpu.make_async_remote_copy(
+            rsrc.at[i], rrcv.at[i], rr_s.at[i], rr_r, device_id=(w, h * 2 + c), device_id_type=MESH
+        )
+
+    far_copy(0, up).start()
+    far_copy(1, down).start()
+    gath_1.direct(1)
+    gath_1.direct(2)
+    gath_0.direct(1)
+    gath_0.direct(2)
     gath_0.direct(3)
     gath_0.direct(4)
     gath_1.ring_b(1)

time: 66.2 us -> 65.1 us (0.983)
  Pallas kernels: 63.8 us -> 62.5 us
    pallas_call x1, Pallas kernels: 63.8 us -> 62.5 us  [per_device(): pl.pallas_call(kernel, out_shape=(pltpu.VMEM((fb, rl), BF16), pltpu.VMEM(...]
where the time goes in v4:
time: 65.1 us; the launch traced here: 64.8 us
  Pallas kernels  62.5 us (96%)
  local copies, waits for them, and re-layouts  1.66 us (3%)
    pallas_call x1, Pallas kernels, per_device(): pl.pallas_call(kernel, out_shape=(pltpu.VMEM((fb, rl), BF16), pltpu.VMEM(...  62.5 us
    unnamed x2, local copies, waits for them, and re-layouts  1.66 us

profile of v4, /device:TPU:1, one launch (start us, length us, event | category | flops | bytes accessed | tf_op | source)
XLA Modules:
  0.0 64.8 jit_solution(12306977289373897255)
XLA Ops:
  0.6 62.5 %merge_step.1 = (bf16[580,1024]{1,0:T(8,128)(2,1)S(1)}, bf16[64,580]{1,0:T(8,128)(2,1)S(1)}) custom-call(s32[1,128]{1,0:T(1,128)} %tok_h.1, s32[64]{0:T(128)} %owner_h.1, bf16[1,128,1024]{2,1,0:T(8,128)(2,1)} %cache_h.1, bf16[1,4640,128]{2,1,0:T(8,128)(2,1)} %bitcast.5, f32[1,16,1024]{2,1,0:T(8,128)} %ab_h.1, f32[1,16,1024]{2,1,0:T(8,128)} %fb_h.1, ...), custom_call_target="tpu_custom_call" | custom-call | tf_op jit(solution)/shard_map/merge_step/pallas_call | solution.py:654
  63.1 1.0 %copy.16 = bf16[1024,580]{0,1:T(8,128)(2,1)} copy(bf16[1024,580]{0,1:T(8,128)(2,1)S(1)} %bitcast.3) | data formatting | bytes 2375680
  64.2 0.6 copy.17
